TPU v7x, 32 devices: a whole 2x2x4 slice. The times are simulated.
32 devices in a mesh: prow: 4 (over x, core), pcol: 8 (over z, y).
Axes of the slice: x: 2, y: 2, z: 4, core: 2. Of those that a mesh axis runs over, the one named last changes fastest.
Arguments:
- coords: int32 [3, 8192], P(None, ('prow', 'pcol')), may hold values from 0 to 1023
- block_map: int32 [64], replicated, may hold values from 0 to 63, each once
- pattern: int32 [2, 64], replicated, may hold values 0 or 1
Outputs:
- factor: float32 [16, 4, 128, 8, 8, 128], P(None, 'prow', None, None, 'pcol')
Inputs may be any that keep to these rules, and one draw needn't show every extreme that they name: `block_map`: every block number appears once.
All inputs are finite; a program needn't handle non-finite values.
Results may differ from a plain program's by a relative error of at most 0.0001.
Values sent between devices are 32-bit elements; how exact they have to be, the bound alone decides.
No kernel may reach another device: no remote copies, remote signals or barrier semaphores. Data moves between devices by JAX's collectives and lax.ppermute only.
A program may use at most 128 MiB of HBM per device.

v0:
```python
import functools

import jax
import jax.numpy as jnp
from jax import lax
from jax.experimental import pallas as pl
from jax.experimental.pallas import tpu as pltpu
from jax.sharding import PartitionSpec as P

BLOCK = 128
SNODE_BLOCKS = 4
PANELS = 2
LEAD = PANELS * SNODE_BLOCKS
WIDTH = SNODE_BLOCKS * BLOCK

spread_factor = 89.0
scale_gain = 8.0
grid_step = 1024.0

LOW, HIGH = 0.98, 66.0

f32 = jnp.float32
bf16 = jnp.bfloat16
NN = (((1,), (0,)), ((), ()))
NT = (((1,), (1,)), ((), ()))
TN = (((0,), (0,)), ((), ()))
FEATURES = 32
VMEM_BYTES = 60 * 1024 * 1024


def mm(a, b, dims):
    return lax.dot_general(a, b, dims, preferred_element_type=f32)


def split(a):
    high = a.astype(bf16)
    low = (a - high.astype(f32)).astype(bf16)
    return high, low


def dot1(a, b, dims=NN):
    return mm(a.astype(bf16), b.astype(bf16), dims)


def mm3(a_high, a_low, b_high, b_low, dims):
    rows = a_high.shape[0]
    both = mm(jnp.concatenate([a_high, a_low], 0), b_high, dims)
    return (both[:rows] + both[rows:]) + mm(a_high, b_low, dims)


def dot3(a, b, dims=NN):
    a_high, a_low = split(a)
    b_high, b_low = split(b)
    return mm3(a_high, a_low, b_high, b_low, dims)


def eye(n):
    return (lax.broadcasted_iota(jnp.int32, (n, n), 0) == lax.broadcasted_iota(jnp.int32, (n, n), 1)).astype(f32)


def newton(blocks, n, beside):
    first = 2 / (LOW + HIGH)
    rho = (HIGH - LOW) / (HIGH + LOW)
    one = eye(n)
    step = 2 / (2 - rho * rho)
    rho = rho * rho / (2 - rho * rho)
    found = [(2 * step * first) * one - (step * first * first) * a for a in blocks]
    for at in range(5):
        dot = dot1 if at < 2 else dot3
        step = 2 / (2 - rho * rho) if at < 4 else 1.0
        rho = rho * rho / (2 - rho * rho)
        rest = [(2 * one) - dot(a, x) for a, x in zip(blocks, found)]
        next(beside, None)
        found = [step * dot(x, e) for x, e in zip(found, rest)]
        next(beside, None)
    return found


def chains(work, count, per_step, beside):
    sub = lax.broadcasted_iota(jnp.int32, (8, BLOCK), 0)
    lane = lax.broadcasted_iota(jnp.int32, (8, BLOCK), 1)
    zero = jnp.zeros((8, BLOCK), f32)

    def strip(step, part):
        n = step * per_step + part
        at = n * 8
        rows = pl.ds(pl.multiple_of(at, 8), 8)
        beside(step, part)
        state = []
        for b in range(count):
            r = work[b][rows, 0:BLOCK]
            y = work[b][rows, BLOCK : 2 * BLOCK]
            turned = pltpu.roll(r, lax.rem(BLOCK - at, BLOCK), 1)
            c = [jnp.broadcast_to(turned[:, k : k + 1], (8, BLOCK)) for k in range(8)]
            state.append([r, y, c])
        for k in range(8):
            for b in range(count):
                r, y, c = state[b]
                inv = lax.rsqrt(c[k][k : k + 1, :])
                column = c[k] * inv
                below = jnp.where(sub > k, column, 0.0)
                r_row = r[k : k + 1] * inv
                y_row = y[k : k + 1] * inv
                r = jnp.where(sub == k, r_row, r - below * r_row)
                y = jnp.where(sub == k, y_row, y - below * y_row)
                for m in range(k + 1, 8):
                    c[m] = c[m] - below * column[m : m + 1, :]
                state[b] = [r, y, c]
        later = lane >= at + 8
        for b in range(count):
            r, y, _ = state[b]
            work[b][rows, 0:BLOCK] = r
            work[b][rows, BLOCK : 2 * BLOCK] = y
            r_high = r.astype(bf16).astype(f32)
            y_high = y.astype(bf16).astype(f32)
            high = jnp.concatenate([r_high, y_high], 1)
            low = jnp.concatenate([r - r_high, y - y_high], 1)
            left_high = jnp.where(later, r_high, 0.0)
            left_low = jnp.where(later, r - r_high, 0.0)
            left = jnp.concatenate([left_high, left_high, left_low, zero], 0).astype(bf16)
            right = jnp.concatenate([high, low, high, jnp.concatenate([zero, zero], 1)], 0).astype(bf16)
            work[b][...] = work[b][...] - mm(left, right, TN)

    def strips(step, carry):
        for n in range(per_step):
            strip(step, n)
        return carry

    lax.fori_loop(0, BLOCK // 8 // per_step, strips, 0)


def factor_diagonal(a_ref, x_ref, work, beside_newton, per_step, beside_strip):
    half = 2 * BLOCK
    rows = lax.broadcasted_iota(jnp.int32, (BLOCK, BLOCK), 0)
    cols = lax.broadcasted_iota(jnp.int32, (BLOCK, BLOCK), 1)
    lower = cols <= rows
    a11 = a_ref[0:half, 0:half]
    a21 = a_ref[half:, 0:half]
    s2 = a_ref[half:, half:] - dot3(dot3(a21, newton([a11], half, beside_newton)[0]), a21, NT)
    corner = [a11[0:BLOCK, 0:BLOCK], s2[0:BLOCK, 0:BLOCK]]
    side = [a11[BLOCK:, 0:BLOCK], s2[BLOCK:, 0:BLOCK]]
    last = [a11[BLOCK:, BLOCK:], s2[BLOCK:, BLOCK:]]
    inverse = newton(corner, BLOCK, beside_newton)
    for i in range(2):
        work[2 * i][:, 0:BLOCK] = corner[i]
        work[2 * i + 1][:, 0:BLOCK] = last[i] - dot3(dot3(side[i], inverse[i]), side[i], NT)
    for b in range(4):
        work[b][:, BLOCK:] = eye(BLOCK)
    for _ in beside_newton:
        pass
    chains(work, 4, per_step, beside_strip)
    for i in range(2):
        at = half * i
        xa = jnp.where(lower, work[2 * i][:, BLOCK:], 0.0)
        xb = jnp.where(lower, work[2 * i + 1][:, BLOCK:], 0.0)
        l21 = dot3(side[i], xa, NT)
        x_ref[at : at + BLOCK, at : at + BLOCK] = xa
        x_ref[at : at + BLOCK, at + BLOCK : at + half] = jnp.zeros((BLOCK, BLOCK), f32)
        x_ref[at + BLOCK : at + half, at : at + BLOCK] = -dot3(xb, dot3(l21, xa))
        x_ref[at + BLOCK : at + half, at + BLOCK : at + half] = xb
    x11 = x_ref[0:half, 0:half]
    x22 = x_ref[half:, half:]
    l21 = dot3(a21, x11, NT)
    x_ref[half:, 0:half] = -dot3(x22, dot3(l21, x11))
    x_ref[0:half, half:] = jnp.zeros((half, half), f32)


def pieces(point):
    low = (point & 255).astype(f32)
    mid = ((point >> 8) & 255).astype(f32)
    top = (point >> 16).astype(f32)
    return low, mid, top


def left_features(point):
    low, mid, top = pieces(point)
    norm = lax.broadcasted_iota(jnp.int32, point.shape, 0) == 3
    one = jnp.ones_like(low)
    zero = jnp.zeros_like(low)
    return jnp.concatenate(
        [low, jnp.where(norm, one, low), mid, jnp.where(norm, one, mid), top, jnp.where(norm, one, zero), zero, zero], 0
    ).astype(bf16)


def right_features(point):
    low, mid, top = pieces(point)
    norm = lax.broadcasted_iota(jnp.int32, point.shape, 0) == 3
    one = jnp.ones_like(low)
    zero = jnp.zeros_like(low)
    return jnp.concatenate(
        [
            jnp.where(norm, one, -2.0 * low),
            jnp.where(norm, low, -512.0 * mid),
            jnp.where(norm, 256.0 * one, -512.0 * low),
            jnp.where(norm, 256.0 * mid, -131072.0 * mid),
            jnp.where(norm, 65536.0 * one, zero),
            jnp.where(norm, 65536.0 * top, zero),
            zero,
            zero,
        ],
        0,
    ).astype(bf16)


def shape_of(radius):
    unit = 1.0 / (grid_step * radius)
    shift = 9.0 / (35.0 * unit)
    return {"reach": 1.0 / unit, "shift": shift, "bias": 3.0 / (35.0 * unit * unit) - shift * shift, "gain": 35.0 / 3.0 * unit**8}


def wendland(dist_sq, shape):
    dist = dist_sq * lax.rsqrt(jnp.maximum(dist_sq, 1.0))
    rest = jnp.maximum(shape["reach"] - dist, 0.0)
    rest_sq = rest * rest
    moved = dist + shape["shift"]
    return (rest_sq * rest_sq) * (rest_sq * (moved * moved + shape["bias"]))


def member(panel_at, block, pattern):
    first = panel_at * SNODE_BLOCKS
    own = (block >= first) & (block < first + SNODE_BLOCKS)
    return jnp.where(own, 1, jnp.where(block < first, 0, pattern[panel_at, block]))


def weight(row, col, pattern):
    value = (row == col).astype(jnp.int32)
    for panel_at in range(PANELS):
        value = value + member(panel_at, row, pattern) * member(panel_at, col, pattern)
    return value.astype(f32)


SCAN = 4
GROUP = 8
UNITS = 32
FIRSTS = 4
CHUNK = 4


def sums_kernel(shape, per, block_map, pattern, points, out, left, lists, weights):
    nblocks = points.shape[0]
    me = lax.axis_index("prow") * lax.axis_size("pcol") + lax.axis_index("pcol")
    own = [block_map[me * per + b] for b in range(per)]
    right = [right_features(points[me * per + b]) for b in range(per)]

    def scan_block(m, counts):
        left[m] = left_features(points[m])
        after = []
        for b in range(per):
            value = weight(own[b], block_map[m], pattern)
            lists[b, counts[b]] = m
            weights[b, counts[b]] = value * shape["gain"]
            after.append(counts[b] + (value > 0).astype(jnp.int32))
        return tuple(after)

    def scan_blocks(step, counts):
        for n in range(SCAN):
            counts = scan_block(step * SCAN + n, counts)
        return counts

    counts = lax.fori_loop(0, nblocks // SCAN, scan_blocks, (0,) * per)
    for b in range(per):
        for g in range(GROUP):
            lists[b, counts[b] + g] = 0
            weights[b, counts[b] + g] = 0.0

    for b in range(per):

        def group(step, total):
            parts = []
            for g in range(GROUP):
                at = step * GROUP + g
                value = wendland(mm(left[lists[b, at]], right[b], TN), shape)
                parts.append(jnp.sum(value.reshape(BLOCK // 8, 8, BLOCK), axis=0) * weights[b, at])
            return total + functools.reduce(lambda x, y: x + y, parts)

        total = lax.fori_loop(0, (counts[b] + GROUP - 1) // GROUP, group, jnp.zeros((8, BLOCK), f32))
        row = jnp.sum(total, axis=0, keepdims=True)
        for d in range(out.shape[0]):
            out[d, b : b + 1, :] = row


def spread_kernel(per, coords, out):
    for b in range(per):
        point = coords[:, b * BLOCK : (b + 1) * BLOCK]
        norm = jnp.sum(point * point, axis=0, keepdims=True)
        point = jnp.concatenate([point, norm], 0)
        for d in range(out.shape[0]):
            out[d, b] = point


def panels_kernel(
    shape, rows_n, cols_n, block_map, pattern, points, totals, out,
    inverse, table, place, units, firsts, panel, high, low, left, right_lead, right_cols, scale_rows, scale_lead, scale_cols,
    diagonal, x_high, x_low, x_full, stage, sems, *work,
):
    nblocks = points.shape[0]
    row_count = nblocks // rows_n
    col_count = nblocks // cols_n
    prow_at = lax.axis_index("prow")
    pcol_at = lax.axis_index("pcol")
    col_base = row_count
    next_base = row_count + col_count
    lead_base = next_base + SNODE_BLOCKS
    slots = lead_base + SNODE_BLOCKS
    lead_rows = LEAD // rows_n

    def invert(m, carry):
        inverse[block_map[m]] = m
        return carry

    lax.fori_loop(0, nblocks, invert, 0)

    def block_rows(slot):
        return pl.ds(pl.multiple_of(slot * BLOCK, BLOCK), BLOCK)

    def pair_rows(slot):
        return pl.ds(pl.multiple_of(slot * BLOCK, 2 * BLOCK), 2 * BLOCK)

    def chunk_rows(slot):
        return pl.ds(pl.multiple_of(slot * BLOCK, CHUNK * BLOCK), CHUNK * BLOCK)

    def scale_of(m):
        return scale_gain * lax.rsqrt(1.0 + totals[pl.ds(m, 1), :])

    def prepare(slot):
        m = inverse[table[slot]]
        left[slot] = left_features(points[m])
        scale_rows[slot] = jnp.broadcast_to(scale_of(m), (BLOCK, BLOCK)).T

    def prepare_lead(j):
        m = inverse[j]
        half, at = divmod(j, SNODE_BLOCKS)
        right_lead[j] = right_features(points[m])
        scale_lead[half, at : at + 1, :] = scale_of(m)

    def prepare_col(k):
        m = inverse[table[col_base + k]]
        right_cols[k // 2, :, k % 2 * BLOCK : (k % 2 + 1) * BLOCK] = right_features(points[m])
        scale_cols[k : k + 1, :] = scale_of(m)

    def coupled(slot, half, j):
        value = wendland(mm(left[slot], right_lead[half * SNODE_BLOCKS + j], TN), shape)
        scale = scale_lead[half, j : j + 1, :] * (weight(table[slot], half * SNODE_BLOCKS + j, pattern) * shape["gain"])
        return value * scale_rows[slot] * scale

    def couple(at, j):
        unit = units[at]
        slot = unit // 2
        half = unit % 2
        lanes = pl.ds(pl.multiple_of(half * WIDTH + j * BLOCK, BLOCK), BLOCK)
        panel[block_rows(slot), lanes] = coupled(slot, half, j)

    for j in range(SNODE_BLOCKS):
        table[next_base + j] = SNODE_BLOCKS + j
        table[lead_base + j] = j
    for j in range(SNODE_BLOCKS):
        prepare(lead_base + j)
        prepare_lead(j)
    for i in range(SNODE_BLOCKS):
        for j in range(SNODE_BLOCKS):
            value = coupled(lead_base + i, 0, j)
            diagonal[i * BLOCK : (i + 1) * BLOCK, j * BLOCK : (j + 1) * BLOCK] = value + eye(BLOCK) if i == j else value

    def sort(base, blocks, lead):
        kinds = []
        first = second = jnp.int32(0)
        for g, at in blocks:
            in_first = member(0, g, pattern) > 0
            in_second = member(1, g, pattern) > 0
            dead = g < LEAD
            kind = jnp.where(dead, 2, jnp.where(in_first, 0, jnp.where(in_second, 1, 2)))
            kinds.append(kind)
            first = first + (kind == 0).astype(jnp.int32)
            second = second + (kind == 1).astype(jnp.int32)
        spots = [base + lead, base + lead + first, base + lead + first + second]
        for (g, at), kind in zip(blocks, kinds):
            spot = jnp.where(kind == 0, spots[0], jnp.where(kind == 1, spots[1], spots[2]))
            table[spot] = g
            place[spot] = at
            for n in range(3):
                spots[n] = spots[n] + (kind == n).astype(jnp.int32)
        return lead + first, lead + first + second

    for i in range(lead_rows):
        table[i] = i * rows_n + prow_at
        place[i] = i
    rows_first, rows_both = sort(0, [(i * rows_n + prow_at, i) for i in range(lead_rows, row_count)], lead_rows)
    cols_first, cols_both = sort(col_base, [(k * cols_n + pcol_at, k) for k in range(col_count)], 0)
    def whole(n):
        return (n + CHUNK - 1) // CHUNK * CHUNK

    count = jnp.int32(0)
    for base, size, ends in ((next_base, SNODE_BLOCKS, (SNODE_BLOCKS,) * PANELS), (0, row_count, (rows_first, rows_both)), (col_base, col_count, (cols_first, cols_both))):
        for at in range(size):
            for half in range(PANELS):
                units[count] = 2 * (base + at) + half
                count = count + jnp.int32(at < ends[half])
    for n in range(UNITS):
        units[count + n] = 2 * lead_base + 1

    first_count = jnp.int32(0)
    for base, size, used in ((0, row_count, rows_first), (col_base, col_count, cols_first)):
        for c in range(0, size, CHUNK):
            firsts[first_count] = base + c
            first_count = first_count + (c < used).astype(jnp.int32)
    for n in range(FIRSTS):
        firsts[first_count + n] = lead_base

    def run(parts, count):
        for n in range(count):
            for part in parts[len(parts) * n // count : len(parts) * (n + 1) // count]:
                part()
            yield

    parts = [functools.partial(prepare_lead, j) for j in range(SNODE_BLOCKS, LEAD)]
    parts += [functools.partial(prepare, slot) for slot in range(lead_base)]
    parts += [functools.partial(prepare_col, k) for k in range(col_count)]

    def couple_beside(step, part):
        n = 2 * step + part
        for unit in range(2):
            for j in range(SNODE_BLOCKS):
                couple(2 * n + unit, j)

    factor_diagonal(diagonal, x_full, work, run(parts, 20), 2, couple_beside)
    x_high[...], x_low[...] = split(x_full[...])

    def couple_more(step, carry):
        for n in range(2):
            for j in range(SNODE_BLOCKS):
                couple(UNITS + 2 * step + n, j)
        return carry

    lax.fori_loop(0, (jnp.maximum(count - UNITS, 0) + 1) // 2, couple_more, 0)
    for base, ends in ((0, (rows_first, rows_both)), (col_base, (cols_first, cols_both))):
        for half, end in enumerate(ends):

            def clear(slot, carry, half=half):
                panel[block_rows(slot), half * WIDTH : (half + 1) * WIDTH] = jnp.zeros((BLOCK, WIDTH), f32)
                return carry

            lax.fori_loop(base + end, base + whole(end), clear, 0)
    for i in range(lead_rows):
        at = slice(i * BLOCK, (i + 1) * BLOCK)
        lanes = pl.ds(pl.multiple_of((i * rows_n + prow_at) * BLOCK, BLOCK), BLOCK)
        panel[at, lanes] = panel[at, lanes] + eye(BLOCK)

    middle = WIDTH // 2

    def solve(at, first):
        a_high, a_low = split(panel[at, first : first + WIDTH])
        for begin, end in ((0, middle), (middle, WIDTH)):
            part = mm3(a_high[:, :end], a_low[:, :end], x_high[begin:end, :end], x_low[begin:end, :end], NT)
            lanes = slice(first + begin, first + end)
            panel[at, lanes] = part
            high[at, lanes], low[at, lanes] = split(part)

    next_rows = slice(next_base * BLOCK, lead_base * BLOCK)
    solve(next_rows, 0)

    def subtract(at, out_ref, out_at):
        for lanes in (slice(0, middle), slice(middle, WIDTH)):
            rows = slice(next_base * BLOCK + lanes.start, next_base * BLOCK + lanes.stop)
            done = mm3(high[at, :WIDTH], low[at, :WIDTH], high[rows, :WIDTH], low[rows, :WIDTH], NT)
            from_at = slice(WIDTH + lanes.start, WIDTH + lanes.stop)
            if out_ref is panel:
                panel[at, from_at] = panel[at, from_at] - done
            else:
                out_ref[out_at, lanes] = panel[at, from_at] - done

    subtract(next_rows, diagonal, slice(0, WIDTH))
    for j in range(SNODE_BLOCKS):
        at = slice(j * BLOCK, (j + 1) * BLOCK)
        diagonal[at, at] = diagonal[at, at] + eye(BLOCK)

    def first_solve(n):
        solve(chunk_rows(firsts[n]), 0)

    def first_subtract(n):
        subtract(chunk_rows(firsts[n]), panel, None)

    def first_beside(step, part):
        if part == 0:
            first_solve(step)
        if part == 2:
            first_subtract(step)

    factor_diagonal(diagonal, x_full, work, iter(()), 4, first_beside)

    def first_more(n, carry):
        first_solve(n)
        first_subtract(n)
        return carry

    lax.fori_loop(FIRSTS, first_count, first_more, 0)
    x_high[...], x_low[...] = split(x_full[...])
    row_chunks = whole(rows_both) // CHUNK

    def second(c, carry):
        slot = jnp.where(c < row_chunks, CHUNK * c, col_base + CHUNK * (c - row_chunks))
        solve(chunk_rows(slot), WIDTH)
        return carry

    lax.fori_loop(0, row_chunks + whole(cols_both) // CHUNK, second, 0)
    for i in range(lead_rows):
        if i * rows_n < SNODE_BLOCKS:

            @pl.when(i * rows_n + prow_at < SNODE_BLOCKS)
            def _(i=i):
                panel[i * BLOCK : (i + 1) * BLOCK, WIDTH:] = jnp.zeros((BLOCK, WIDTH), f32)

    per_slot = BLOCK * col_count
    row_live = whole(rows_both) // CHUNK
    row_two = whole(rows_first) // CHUNK
    col_live = (cols_both + 1) // 2
    col_two = (cols_first + 1) // 2

    def copies_out(step, half):
        made = []
        for q in range(CHUNK):
            at = pl.multiple_of(place[CHUNK * step + q] * per_slot, per_slot)
            made.append(
                pltpu.make_async_copy(stage.at[half, pl.ds(q * per_slot, per_slot), :], out.at[pl.ds(at, per_slot), :], sems.at[half, q])
            )
        return made

    def trail(step, carry):
        half = step % 2

        @pl.when(step >= 2)
        def _():
            for copy in copies_out(step - 2, half):
                copy.wait()

        def spots(q, k):
            return pl.ds(q * per_slot + k, BLOCK, stride=col_count)

        def tiles(c, carry):
            live = (step < row_live) & (c < col_live)
            two = (step < row_two) & (c < col_two)
            row_at = chunk_rows(CHUNK * step)
            col_at = pair_rows(col_base + 2 * c)

            def body(first):
                tiles = []
                for q in range(CHUNK):
                    slot = CHUNK * step + q
                    value = wendland(mm(left[slot], right_cols[c], TN), shape)
                    for e in range(2):
                        spot = col_base + 2 * c + e
                        factor = scale_cols[pl.ds(2 * c + e, 1), :] * (weight(table[slot], table[spot], pattern) * shape["gain"])
                        tiles.append(value[:, e * BLOCK : (e + 1) * BLOCK] * scale_rows[slot] * factor)
                update = mm3(high[row_at, first:], low[row_at, first:], high[col_at, first:], low[col_at, first:], NT)
                for q in range(CHUNK):
                    for e in range(2):
                        spot = col_base + 2 * c + e
                        tile = tiles[2 * q + e] - update[q * BLOCK : (q + 1) * BLOCK, e * BLOCK : (e + 1) * BLOCK]
                        stage[half, spots(q, place[spot]), :] = tile

            @pl.when(live & two)
            def _():
                body(0)

            @pl.when(live & jnp.logical_not(two))
            def _():
                body(WIDTH)

            @pl.when(jnp.logical_not(live))
            def _():
                for q in range(CHUNK):
                    for e in range(2):
                        stage[half, spots(q, place[col_base + 2 * c + e]), :] = jnp.zeros((BLOCK, BLOCK), f32)

            return carry

        lax.fori_loop(0, col_count // 2, tiles, 0)

        @pl.when(step == 0)
        def _():
            for q in range(lead_rows):
                for k in range(col_count):
                    stage[half, spots(q, k), :] = jnp.zeros((BLOCK, BLOCK), f32)

        for q in range(CHUNK):
            slot = CHUNK * step + q
            g = table[slot]
            k_same = g // cols_n
            here = (k_same * cols_n + pcol_at == g) & (g >= LEAD)
            same = spots(q, k_same)

            @pl.when(here & (slot >= rows_both))
            def _(slot=slot, g=g, same=same):
                m = inverse[g]
                value = wendland(mm(left[slot], right_features(points[m]), TN), shape)
                factor = scale_gain * lax.rsqrt(1.0 + totals[pl.ds(m, 1), :]) * (weight(g, g, pattern) * shape["gain"])
                stage[half, same, :] = value * scale_rows[slot] * factor

            @pl.when(here)
            def _(same=same):
                stage[half, same, :] = stage[half, same, :] + eye(BLOCK)

            for k in range(col_count):
                if k * cols_n < LEAD:
                    j = k * cols_n + pcol_at

                    filled = slot < jnp.where(j < SNODE_BLOCKS, rows_first, rows_both)

                    @pl.when((j < LEAD) & filled)
                    def _(k=k, j=j, q=q, slot=slot):
                        where = pl.ds(pl.multiple_of(j * BLOCK, BLOCK), BLOCK)
                        stage[half, spots(q, k), :] = panel[block_rows(slot), where]

                    @pl.when((j < LEAD) & jnp.logical_not(filled))
                    def _(k=k, q=q):
                        stage[half, spots(q, k), :] = jnp.zeros((BLOCK, BLOCK), f32)

        for copy in copies_out(step, half):
            copy.start()
        return carry

    steps = row_count // CHUNK
    lax.fori_loop(0, steps, trail, 0)
    for step in range(max(steps - 2, 0), steps):
        for copy in copies_out(step, step % 2):
            copy.wait()


def local(coords, block_map, pattern):
    rows_n = lax.axis_size("prow")
    cols_n = lax.axis_size("pcol")
    devices = rows_n * cols_n
    nblocks = block_map.shape[0]
    per = nblocks // devices
    row_count = nblocks // rows_n
    col_count = nblocks // cols_n
    radius = (spread_factor / (nblocks * BLOCK)) ** (1.0 / 3.0)
    slots = row_count + col_count + LEAD
    rows_kept = (slots - SNODE_BLOCKS + CHUNK) * BLOCK
    axes = ("prow", "pcol")
    smem = pl.BlockSpec(memory_space=pltpu.SMEM)
    vmem = pl.BlockSpec(memory_space=pltpu.VMEM)
    params = pltpu.CompilerParams(vmem_limit_bytes=VMEM_BYTES)
    shape = shape_of(radius)
    mine = pl.pallas_call(
        functools.partial(spread_kernel, per),
        out_shape=jax.ShapeDtypeStruct((devices, per, 4, BLOCK), jnp.int32),
        in_specs=[vmem],
        out_specs=vmem,
        name="spread",
    )(coords)
    points = lax.all_to_all(mine, axes, 0, 0, tiled=True).reshape(nblocks, 4, BLOCK)
    sums = pl.pallas_call(
        functools.partial(sums_kernel, shape, per),
        out_shape=jax.ShapeDtypeStruct((devices, per, BLOCK), f32),
        in_specs=[smem, smem, vmem],
        out_specs=vmem,
        scratch_shapes=[
            pltpu.VMEM((nblocks, FEATURES, BLOCK), bf16),
            pltpu.SMEM((per, nblocks + GROUP), jnp.int32),
            pltpu.SMEM((per, nblocks + GROUP), f32),
        ],
        compiler_params=params,
        name="sums",
    )(block_map, pattern, points)
    totals = lax.all_to_all(sums, axes, 0, 0, tiled=True).reshape(nblocks, BLOCK)
    out = pl.pallas_call(
        functools.partial(panels_kernel, shape, rows_n, cols_n),
        out_shape=jax.ShapeDtypeStruct((row_count * BLOCK * col_count, BLOCK), f32),
        in_specs=[smem, smem, vmem, vmem],
        out_specs=pl.BlockSpec(memory_space=pl.ANY),
        scratch_shapes=[
            pltpu.SMEM((nblocks,), jnp.int32),
            pltpu.SMEM((slots,), jnp.int32),
            pltpu.SMEM((slots,), jnp.int32),
            pltpu.SMEM((2 * slots + UNITS,), jnp.int32),
            pltpu.SMEM((slots + FIRSTS,), jnp.int32),
            pltpu.VMEM((rows_kept, PANELS * WIDTH), f32),
            pltpu.VMEM((rows_kept, PANELS * WIDTH), bf16),
            pltpu.VMEM((rows_kept, PANELS * WIDTH), bf16),
            pltpu.VMEM((slots, FEATURES, BLOCK), bf16),
            pltpu.VMEM((LEAD, FEATURES, BLOCK), bf16),
            pltpu.VMEM((col_count // 2, FEATURES, 2 * BLOCK), bf16),
            pltpu.VMEM((slots, BLOCK, BLOCK), f32),
            pltpu.VMEM((PANELS, SNODE_BLOCKS, BLOCK), f32),
            pltpu.VMEM((col_count, BLOCK), f32),
            pltpu.VMEM((WIDTH, WIDTH), f32),
            pltpu.VMEM((WIDTH, WIDTH), bf16),
            pltpu.VMEM((WIDTH, WIDTH), bf16),
            pltpu.VMEM((WIDTH, WIDTH), f32),
            pltpu.VMEM((2, CHUNK * BLOCK * col_count, BLOCK), f32),
            pltpu.SemaphoreType.DMA((2, CHUNK)),
        ]
        + [pltpu.VMEM((BLOCK, 2 * BLOCK), f32)] * 4,
        compiler_params=params,
        name="panels",
    )(block_map, pattern, points, totals)
    return out.reshape(row_count, 1, BLOCK, col_count, 1, BLOCK)


def solution(mesh):
    placed = (P(None, ("prow", "pcol")), P(), P())
    return jax.shard_map(
        local,
        mesh=mesh,
        in_specs=placed,
        out_specs=P(None, "prow", None, None, "pcol", None),
        check_vma=False,
    )
```

profile of v0, /device:TPU:0, one launch (start us, length us, event | category | flops | bytes accessed | tf_op | source)
XLA Modules:
  0.0 101.5 jit_solution(16358308885828644266)
XLA Ops:
  0.0 1.4 %spread.1 = s32[32,2,4,128]{3,2,1,0:T(4,128)} custom-call(s32[3,256]{1,0:T(4,128)} %coords.1), custom_call_target="tpu_custom_call" | custom-call | tf_op jit(solution)/shard_map/spread/pallas_call | solution.py:644
  1.4 15.2 %all_to_all.10 = s32[32,2,4,128]{3,2,1,0:T(4,128)} all-to-all(s32[32,2,4,128]{3,2,1,0:T(4,128)} %spread.1), channel_id=1, replica_groups=mesh['prow'=4,'pcol'=8] {'prow','pcol'}, dimensions={0} | all-to-all | bytes 262144 | tf_op jit(solution)/shard_map/all_to_all | solution.py:651
  16.6 8.1 %sums.1 = f32[32,2,128]{2,1,0:T(2,128)} custom-call(s32[64]{0:T(128)} %block_map.3, s32[2,64]{1,0:T(2,128)} %pattern.3, s32[64,4,128]{2,1,0:T(4,128)} %bitcast.5), custom_call_target="tpu_custom_call" | custom-call | tf_op jit(solution)/shard_map/sums/pallas_call | solution.py:652
  24.7 10.4 %all_to_all.11 = f32[32,2,128]{2,1,0:T(2,128)} all-to-all(f32[32,2,128]{2,1,0:T(2,128)} %sums.1), channel_id=1, replica_groups=mesh['prow'=4,'pcol'=8] {'prow','pcol'}, dimensions={0} | all-to-all | bytes 65536 | tf_op jit(solution)/shard_map/all_to_all | solution.py:665
  35.2 66.1 %panels.1 = f32[16384,128]{1,0:T(8,128)} custom-call(s32[64]{0:T(128)} %block_map.3, s32[2,64]{1,0:T(2,128)} %pattern.3, s32[64,4,128]{2,1,0:T(4,128)} %bitcast.6, f32[64,128]{1,0:T(8,128)} %bitcast.7), custom_call_target="tpu_custom_call" | custom-call | tf_op jit(solution)/shard_map/panels/pallas_call | solution.py:666
where the time goes:
time: 102 us; the launch traced here: 101 us
  Pallas kernels  75.6 us (74%)
  blocking collectives  25.7 us (25%)
    pallas_call x1, Pallas kernels, local(): pl.pallas_call(functools.partial(panels_kernel, shape, rows_n, cols_n), o...  66.1 us
    all_to_all x1, blocking collectives, local(): lax.all_to_all(mine, axes, 0, 0, tiled=True).reshape(nblocks, 4, BLOCK)  15.2 us
    all_to_all x1, blocking collectives, local(): lax.all_to_all(sums, axes, 0, 0, tiled=True).reshape(nblocks, BLOCK)  10.4 us
    pallas_call x1, Pallas kernels, local(): pl.pallas_call(functools.partial(sums_kernel, shape, per), out_shape=jax....  8.11 us

commit v1 on v0

--- a/solution.py
+++ b/solution.py
@@ -290,7 +290,7 @@
 
 def panels_kernel(
     shape, rows_n, cols_n, block_map, pattern, points, totals, out,
-    inverse, table, place, units, firsts, panel, high, low, left, right_lead, right_cols, scale_rows, scale_lead, scale_cols,
+    inverse, table, place, units, firsts, seconds, panel, high, low, left, right_lead, right_cols, scale_rows, scale_lead, scale_cols,
     diagonal, x_high, x_low, x_full, stage, sems, *work,
 ):
     nblocks = points.shape[0]
@@ -361,7 +361,7 @@
             value = coupled(lead_base + i, 0, j)
             diagonal[i * BLOCK : (i + 1) * BLOCK, j * BLOCK : (j + 1) * BLOCK] = value + eye(BLOCK) if i == j else value
 
-    def sort(base, blocks, lead):
+    def sort(base, blocks):
         kinds = []
         first = second = jnp.int32(0)
         for g, at in blocks:
@@ -372,20 +372,21 @@
             kinds.append(kind)
             first = first + (kind == 0).astype(jnp.int32)
             second = second + (kind == 1).astype(jnp.int32)
-        spots = [base + lead, base + lead + first, base + lead + first + second]
+        spots = [base, base + first, base + first + second]
         for (g, at), kind in zip(blocks, kinds):
             spot = jnp.where(kind == 0, spots[0], jnp.where(kind == 1, spots[1], spots[2]))
             table[spot] = g
             place[spot] = at
             for n in range(3):
                 spots[n] = spots[n] + (kind == n).astype(jnp.int32)
-        return lead + first, lead + first + second
-
+        return first, first + second
+
+    real_rows = row_count - lead_rows
     for i in range(lead_rows):
-        table[i] = i * rows_n + prow_at
-        place[i] = i
-    rows_first, rows_both = sort(0, [(i * rows_n + prow_at, i) for i in range(lead_rows, row_count)], lead_rows)
-    cols_first, cols_both = sort(col_base, [(k * cols_n + pcol_at, k) for k in range(col_count)], 0)
+        table[real_rows + i] = i * rows_n + prow_at
+        place[real_rows + i] = i
+    rows_first, rows_both = sort(0, [(i * rows_n + prow_at, i) for i in range(lead_rows, row_count)])
+    cols_first, cols_both = sort(col_base, [(k * cols_n + pcol_at, k) for k in range(col_count)])
     def whole(n):
         return (n + CHUNK - 1) // CHUNK * CHUNK
 
@@ -394,15 +395,21 @@
         for at in range(size):
             for half in range(PANELS):
                 units[count] = 2 * (base + at) + half
-                count = count + jnp.int32(at < ends[half])
+                used = jnp.int32(at < ends[half]) if base or at < real_rows else 1
+                count = count + used
     for n in range(UNITS):
         units[count + n] = 2 * lead_base + 1
 
-    first_count = jnp.int32(0)
-    for base, size, used in ((0, row_count, rows_first), (col_base, col_count, cols_first)):
-        for c in range(0, size, CHUNK):
-            firsts[first_count] = base + c
-            first_count = first_count + (c < used).astype(jnp.int32)
+    def list_chunks(rows, cols, out):
+        count = jnp.int32(0)
+        for base, size, end in ((0, row_count, rows), (col_base, col_count, cols)):
+            for c in range(0, size, CHUNK):
+                out[count] = base + c
+                count = count + (1 if c == row_count - CHUNK and not base else (c < end).astype(jnp.int32))
+        return count
+
+    first_count = list_chunks(rows_first, cols_first, firsts)
+    second_count = list_chunks(rows_both, cols_both, seconds)
     for n in range(FIRSTS):
         firsts[first_count + n] = lead_base
 
@@ -426,22 +433,22 @@
     x_high[...], x_low[...] = split(x_full[...])
 
     def couple_more(step, carry):
-        for n in range(2):
+        for n in range(4):
             for j in range(SNODE_BLOCKS):
-                couple(UNITS + 2 * step + n, j)
+                couple(UNITS + 4 * step + n, j)
         return carry
 
-    lax.fori_loop(0, (jnp.maximum(count - UNITS, 0) + 1) // 2, couple_more, 0)
-    for base, ends in ((0, (rows_first, rows_both)), (col_base, (cols_first, cols_both))):
+    lax.fori_loop(0, (jnp.maximum(count - UNITS, 0) + 3) // 4, couple_more, 0)
+    for base, stop, ends in ((0, real_rows, (rows_first, rows_both)), (col_base, col_count, (cols_first, cols_both))):
         for half, end in enumerate(ends):
 
             def clear(slot, carry, half=half):
                 panel[block_rows(slot), half * WIDTH : (half + 1) * WIDTH] = jnp.zeros((BLOCK, WIDTH), f32)
                 return carry
 
-            lax.fori_loop(base + end, base + whole(end), clear, 0)
+            lax.fori_loop(base + end, base + stop, clear, 0)
     for i in range(lead_rows):
-        at = slice(i * BLOCK, (i + 1) * BLOCK)
+        at = slice((real_rows + i) * BLOCK, (real_rows + i + 1) * BLOCK)
         lanes = pl.ds(pl.multiple_of((i * rows_n + prow_at) * BLOCK, BLOCK), BLOCK)
         panel[at, lanes] = panel[at, lanes] + eye(BLOCK)
 
@@ -494,20 +501,17 @@
 
     lax.fori_loop(FIRSTS, first_count, first_more, 0)
     x_high[...], x_low[...] = split(x_full[...])
-    row_chunks = whole(rows_both) // CHUNK
-
-    def second(c, carry):
-        slot = jnp.where(c < row_chunks, CHUNK * c, col_base + CHUNK * (c - row_chunks))
-        solve(chunk_rows(slot), WIDTH)
+    def second(n, carry):
+        solve(chunk_rows(seconds[n]), WIDTH)
         return carry
 
-    lax.fori_loop(0, row_chunks + whole(cols_both) // CHUNK, second, 0)
+    lax.fori_loop(0, second_count, second, 0)
     for i in range(lead_rows):
         if i * rows_n < SNODE_BLOCKS:
 
             @pl.when(i * rows_n + prow_at < SNODE_BLOCKS)
             def _(i=i):
-                panel[i * BLOCK : (i + 1) * BLOCK, WIDTH:] = jnp.zeros((BLOCK, WIDTH), f32)
+                panel[(real_rows + i) * BLOCK : (real_rows + i + 1) * BLOCK, WIDTH:] = jnp.zeros((BLOCK, WIDTH), f32)
 
     per_slot = BLOCK * col_count
     row_live = whole(rows_both) // CHUNK
@@ -523,6 +527,8 @@
                 pltpu.make_async_copy(stage.at[half, pl.ds(q * per_slot, per_slot), :], out.at[pl.ds(at, per_slot), :], sems.at[half, q])
             )
         return made
+
+    steps = row_count // CHUNK
 
     def trail(step, carry):
         half = step % 2
@@ -575,9 +581,9 @@
 
         lax.fori_loop(0, col_count // 2, tiles, 0)
 
-        @pl.when(step == 0)
+        @pl.when(step == steps - 1)
         def _():
-            for q in range(lead_rows):
+            for q in range(CHUNK - lead_rows, CHUNK):
                 for k in range(col_count):
                     stage[half, spots(q, k), :] = jnp.zeros((BLOCK, BLOCK), f32)
 
@@ -603,7 +609,7 @@
                 if k * cols_n < LEAD:
                     j = k * cols_n + pcol_at
 
-                    filled = slot < jnp.where(j < SNODE_BLOCKS, rows_first, rows_both)
+                    filled = (slot < jnp.where(j < SNODE_BLOCKS, rows_first, rows_both)) | (slot >= real_rows)
 
                     @pl.when((j < LEAD) & filled)
                     def _(k=k, j=j, q=q, slot=slot):
@@ -618,7 +624,6 @@
             copy.start()
         return carry
 
-    steps = row_count // CHUNK
     lax.fori_loop(0, steps, trail, 0)
     for step in range(max(steps - 2, 0), steps):
         for copy in copies_out(step, step % 2):
@@ -674,6 +679,7 @@
             pltpu.SMEM((slots,), jnp.int32),
             pltpu.SMEM((2 * slots + UNITS,), jnp.int32),
             pltpu.SMEM((slots + FIRSTS,), jnp.int32),
+            pltpu.SMEM((slots,), jnp.int32),
             pltpu.VMEM((rows_kept, PANELS * WIDTH), f32),
             pltpu.VMEM((rows_kept, PANELS * WIDTH), bf16),
             pltpu.VMEM((rows_kept, PANELS * WIDTH), bf16),

time: 102 us -> 94.4 us (0.925)
  Pallas kernels: 75.6 us -> 64.6 us
  blocking collectives: 25.7 us -> 28.3 us
    pallas_call x1, Pallas kernels: 66.1 us -> 58.9 us  [local(): pl.pallas_call(functools.partial(panels_kernel, shape, rows_n, cols_n), o...]
    pallas_call x1, Pallas kernels: 8.11 us -> 4.29 us  [local(): pl.pallas_call(functools.partial(sums_kernel, shape, per), out_shape=jax....]
    all_to_all x1, blocking collectives: 10.4 us -> 13.1 us  [local(): lax.all_to_all(sums, axes, 0, 0, tiled=True).reshape(nblocks, BLOCK)]
where the time goes in v1:
time: 94.4 us; the launch traced here: 93.1 us
  Pallas kernels  64.6 us (68%)
  blocking collectives  28.3 us (30%)
    pallas_call x1, Pallas kernels, local(): pl.pallas_call(functools.partial(panels_kernel, shape, rows_n, cols_n), o...  58.9 us
    all_to_all x1, blocking collectives, local(): lax.all_to_all(mine, axes, 0, 0, tiled=True).reshape(nblocks, 4, BLOCK)  15.2 us
    all_to_all x1, blocking collectives, local(): lax.all_to_all(sums, axes, 0, 0, tiled=True).reshape(nblocks, BLOCK)  13.1 us
    pallas_call x1, Pallas kernels, local(): pl.pallas_call(functools.partial(sums_kernel, shape, per), out_shape=jax....  4.29 us

profile of v1, /device:TPU:0, one launch (start us, length us, event | category | flops | bytes accessed | tf_op | source)
XLA Modules:
  0.0 93.1 jit_solution(3578130539123135721)
XLA Ops:
  0.0 1.4 %spread.1 = s32[32,2,4,128]{3,2,1,0:T(4,128)} custom-call(s32[3,256]{1,0:T(4,128)} %coords.1), custom_call_target="tpu_custom_call" | custom-call | tf_op jit(solution)/shard_map/spread/pallas_call | solution.py:649
  1.4 15.2 %all_to_all.10 = s32[32,2,4,128]{3,2,1,0:T(4,128)} all-to-all(s32[32,2,4,128]{3,2,1,0:T(4,128)} %spread.1), channel_id=1, replica_groups=mesh['prow'=4,'pcol'=8] {'prow','pcol'}, dimensions={0} | all-to-all | bytes 262144 | tf_op jit(solution)/shard_map/all_to_all | solution.py:656
  16.6 4.3 %sums.1 = f32[32,2,128]{2,1,0:T(2,128)} custom-call(s32[64]{0:T(128)} %block_map.3, s32[2,64]{1,0:T(2,128)} %pattern.3, s32[64,4,128]{2,1,0:T(4,128)} %bitcast.5), custom_call_target="tpu_custom_call" | custom-call | tf_op jit(solution)/shard_map/sums/pallas_call | solution.py:657
  20.9 13.1 %all_to_all.11 = f32[32,2,128]{2,1,0:T(2,128)} all-to-all(f32[32,2,128]{2,1,0:T(2,128)} %sums.1), channel_id=1, replica_groups=mesh['prow'=4,'pcol'=8] {'prow','pcol'}, dimensions={0} | all-to-all | bytes 65536 | tf_op jit(solution)/shard_map/all_to_all | solution.py:670
  34.0 58.9 %panels.1 = f32[16384,128]{1,0:T(8,128)} custom-call(s32[64]{0:T(128)} %block_map.3, s32[2,64]{1,0:T(2,128)} %pattern.3, s32[64,4,128]{2,1,0:T(4,128)} %bitcast.6, f32[64,128]{1,0:T(8,128)} %bitcast.7), custom_call_target="tpu_custom_call" | custom-call | tf_op jit(solution)/shard_map/panels/pallas_call | solution.py:671
